TPU v7x, 1024 devices: a whole 4x8x16 slice. The times are simulated.
1024 devices in a mesh: fsdp: 256 (over x, z_lo, y, core), ctx: 4 (over z_hi).
Axes of the slice: x: 4, y: 8, z: 16 (z_hi: 4, z_lo: 4; z = z_hi * 4 + z_lo), core: 2. Of those that a mesh axis runs over, the one named last changes fastest.
Arguments:
- hidden_states: bfloat16 [256, 1536, 4096], P('fsdp', 'ctx'), may hold values from -20.4 to 20.4
- qkv_weight: bfloat16 [4096, 768], P('fsdp'), may hold values from -0.09375 to 0.09375
- doc_ids: int32 [256, 1536], P('fsdp', 'ctx'), may hold values from 0 to 1, never falling along the last dimension, each value on 1 to 1344 neighbouring positions
Outputs:
- context: bfloat16 [256, 1536, 512], P('fsdp', 'ctx')
Inputs may be any that keep to these rules, and one draw needn't show every extreme that they name: `doc_ids`: each sequence holds two documents one after the other, numbered 0 then 1, never falling; the first has 192 to 1344 tokens and the second the rest.
All inputs are finite; a program needn't handle non-finite values.
Results may differ from a plain program's by a relative error of at most 0.012.
The roundings to bfloat16 on the way count: a program that leaves them out, or rounds other values in their place, can miss the bound.
Values may be sent and summed in bfloat16 or wider, within the bound.
A program may use at most 32 MiB of HBM per device.

v0:
```python
import math

import jax
import jax.numpy as jnp
from jax import lax
from jax.sharding import PartitionSpec as P

HEADS = 4
HD = 128


THETA = 1000000.0


def shifted(value, axis, steps):
    count = lax.axis_size(axis)
    first, last = (max(0, -steps), min(count, count - steps))
    return lax.ppermute(value, axis, [(source, source + steps) for source in range(first, last)])


def rotary(values_in, positions):
    half_width = values_in.shape[-1] // 2
    frequency = jnp.exp(
        jnp.arange(half_width, dtype=jnp.float32) * (-2.0 * math.log(THETA) / values_in.shape[-1])
    )
    angles = positions * frequency
    cosine = jnp.cos(angles)
    sine_part = jnp.sin(angles)
    lower_half = values_in[..., :half_width]
    upper_half = values_in[..., half_width:]
    return jnp.concatenate(
        [
            lower_half * cosine - upper_half * sine_part,
            upper_half * cosine + lower_half * sine_part,
        ],
        axis=-1,
    )


def body(hidden_states, qkv_weight, doc_ids):
    tokens = hidden_states[0]
    row_count = tokens.shape[0]
    projected = jnp.dot(
        tokens,
        lax.all_gather(qkv_weight, "fsdp", axis=0, tiled=True),
        preferred_element_type=jnp.float32,
    )
    ctx_count = lax.axis_size("ctx")
    ctx_index = lax.axis_index("ctx")
    row_start = ctx_index * row_count
    local_index = jnp.arange(row_count, dtype=jnp.int32)
    query_pos = row_start + local_index
    positions = query_pos.astype(jnp.float32)
    queries = rotary(
        projected[:, : HEADS * HD].reshape(row_count, HEADS, HD), positions[:, None, None]
    ).astype(jnp.bfloat16)
    keys_here = rotary(projected[:, HEADS * HD : (HEADS + 1) * HD], positions[:, None]).astype(
        jnp.bfloat16
    )
    values_here = projected[:, (HEADS + 1) * HD :].astype(jnp.bfloat16)
    docs_wire = doc_ids[0].astype(jnp.bfloat16)
    scale = 1.0 / math.sqrt(HD)

    def attend(state, key_block, value_block, doc_block, key_first):
        running_max, running_sum, running_acc = state
        scores = (
            jnp.einsum("qhd,kd->hqk", queries, key_block, preferred_element_type=jnp.float32)
            * scale
        )
        key_pos = key_first + jnp.arange(key_block.shape[0], dtype=jnp.int32)
        visible = (key_pos[None, :] <= query_pos[:, None]) & (
            doc_block[None, :] == docs_wire[:, None]
        )
        scores = jnp.where(visible[None], scores, -jnp.inf)
        new_max = jnp.maximum(running_max, jnp.max(scores, axis=-1))
        weights = jnp.exp(scores - new_max[..., None])
        factor = jnp.exp(running_max - new_max)
        new_sum = running_sum * factor + jnp.sum(weights, axis=-1)
        update = jnp.einsum(
            "hqk,kd->hqd",
            weights.astype(jnp.bfloat16),
            value_block,
            preferred_element_type=jnp.float32,
        )
        new_acc = running_acc * factor[..., None] + update
        return (new_max, new_sum, new_acc)

    state = (
        jnp.full((HEADS, row_count), -jnp.inf, jnp.float32),
        jnp.zeros((HEADS, row_count), jnp.float32),
        jnp.zeros((HEADS, row_count, HD), jnp.float32),
    )
    state = attend(state, keys_here, values_here, docs_wire, row_start)
    travelling = (keys_here, values_here, docs_wire)
    for rotation in range(1, ctx_count):
        travelling = shifted((travelling[0], travelling[1], travelling[2]), "ctx", 1)
        key_first = (ctx_index - rotation) * row_count
        arrived = travelling

        def take_block(current):
            return attend(current, arrived[0], arrived[1], arrived[2], key_first)

        def keep_block(current):
            return current

        state = lax.cond(rotation <= ctx_index, take_block, keep_block, state)
    context = state[2] / state[1][..., None]
    context = jnp.transpose(context.astype(jnp.bfloat16), (1, 0, 2)).reshape(row_count, HEADS * HD)
    return context[None]


def solution(mesh):
    in_specs = (P("fsdp", "ctx", None), P("fsdp", None), P("fsdp", "ctx"))
    out_specs = P("fsdp", "ctx", None)
    return jax.shard_map(body, mesh=mesh, in_specs=in_specs, out_specs=out_specs, check_vma=False)
```

profile of v0, /device:TPU:448, one launch (start us, length us, event | category | flops | bytes accessed | tf_op | source)
XLA Modules:
  0.0 524.1 jit_solution(12957986975699098648)
XLA Ops:
  6.5 0.0 copy-start
  6.5 0.7 all-gather.2.cloned.1.call-update
  7.3 0.9 convert_reduce_fusion
  8.2 8.2 %collective-permute-start = (bf16[384]{0:T(512)(128)(2,1)S(1)}, bf16[384]{0:T(512)(128)(2,1)S(1)}, u32[]{:S(2)}, u32[]{:S(2)}) collective-permute-start(bf16[384]{0:T(512)(128)(2,1)S(1)} %convert_reduce_fusion), channel_id=1, source_target_pairs={{0,1},{1,2},{2,3},{4,5},{5,6},{6,7},{8,9},{9,10},{10,11},{12,13},{... | collective-permute-start | bytes 2312 | tf_op jit(solution)/shard_map/ppermute | solution.py:18
  16.4 0.0 copy-start.9
  16.4 0.8 compare_and_fusion.3
  17.3 0.4 collective-permute-done
  17.7 8.1 %collective-permute-start.3 = (bf16[384]{0:T(512)(128)(2,1)S(1)}, bf16[384]{0:T(512)(128)(2,1)}, u32[]{:S(2)}, u32[]{:S(2)}) collective-permute-start(bf16[384]{0:T(512)(128)(2,1)S(1)} %collective-permute-done), channel_id=1, source_target_pairs={{0,1},{1,2},{2,3},{4,5},{5,6},{6,7},{8,9},{9,10},{10,11},{12,13},{... | collective-permute-start | bytes 2312 | tf_op jit(solution)/shard_map/ppermute | solution.py:18
  25.8 1.4 collective-permute-done.3
  27.2 8.1 %collective-permute-start.6 = (bf16[384]{0:T(512)(128)(2,1)}, bf16[384]{0:T(512)(128)(2,1)}, u32[]{:S(2)}, u32[]{:S(2)}) collective-permute-start(bf16[384]{0:T(512)(128)(2,1)} %collective-permute-done.3), channel_id=1, source_target_pairs={{0,1},{1,2},{2,3},{4,5},{5,6},{6,7},{8,9},{9,10},{10,11},{12,13},{... | collective-permute-start | bytes 2312 | tf_op jit(solution)/shard_map/ppermute | solution.py:18
  35.3 403.7 %all-gather.2.cloned.1.call-done = bf16[4096,768]{1,0:T(8,128)(2,1)} async-done(((bf16[16,768]{1,0:T(8,128)(2,1)}), bf16[4096,768]{1,0:T(8,128)(2,1)}) %all-gather.2.cloned.1.call-update) | async-done | bytes 6291472 | tf_op jit(solution)/shard_map/all_gather | solution.py:45
  439.0 5.4 %fusion.39 = f32[384,768]{1,0:T(8,128)S(1)} fusion(bf16[4096,768]{1,0:T(8,128)(2,1)} %all-gather.2.cloned.1.call-done, bf16[1,384,4096]{2,1,0:T(8,128)(2,1)S(1)} %copy-done), kind=kOutput, calls=%fused_computation.57 | convolution fusion | flops 2415919104 | bytes 10616832 | tf_op jit(solution)/shard_map/dot_general | solution.py:43
  444.4 0.7 slice.39
  445.1 1.0 slice.30
  446.1 5.3 %collective-permute-start.2 = (bf16[384,128]{1,0:T(8,128)(2,1)}, bf16[384,128]{1,0:T(8,128)(2,1)}, u32[]{:S(2)}, u32[]{:S(2)}) collective-permute-start(bf16[384,128]{1,0:T(8,128)(2,1)} %slice.39), channel_id=1, source_target_pairs={{0,1},{1,2},{2,3},{4,5},{5,6},{6,7},{8,9},{9,10},{10,11},{12,13},{... | collective-permute-start | bytes 294920 | tf_op jit(solution)/shard_map/ppermute | solution.py:18
  451.4 0.8 subtract_convert_fusion.1
  452.2 0.7 pad_maximum_fusion.1
  453.0 3.2 collective-permute-start.1
  456.1 2.3 reshape.338
  458.4 1.8 fusion.57
  460.2 0.0 copy-start.2
  460.3 0.2 subtract_convert_fusion
  460.5 0.2 pad_maximum_fusion
  460.7 0.5 copy-done.2
  461.2 1.4 fusion.43
  462.6 0.5 fusion.42
  463.1 4.2 collective-permute-done.2
  467.3 3.6 collective-permute-start.5
  470.9 14.0 %collective-permute-done.1 = bf16[384,128]{1,0:T(8,128)(2,1)} collective-permute-done((bf16[384,128]{1,0:T(8,128)(2,1)}, bf16[384,128]{1,0:T(8,128)(2,1)}, u32[]{:S(2)}, u32[]{:S(2)}) %collective-permute-start.1) | collective-permute-done | bytes 98336 | tf_op jit(solution)/shard_map/ppermute | solution.py:18
  484.9 1.9 collective-permute-start.4
  486.9 0.2 collective-permute-done.5
  487.0 5.7 %collective-permute-start.8 = (bf16[384,128]{1,0:T(8,128)(2,1)}, bf16[384,128]{1,0:T(8,128)(2,1)}, u32[]{:S(2)}, u32[]{:S(2)}) collective-permute-start(bf16[384,128]{1,0:T(8,128)(2,1)} %collective-permute-done.5), channel_id=1, source_target_pairs={{0,1},{1,2},{2,3},{4,5},{5,6},{6,7},{8,9},{9,10},{10,11},{12,13},{... | collective-permute-start | bytes 294920 | tf_op jit(solution)/shard_map/ppermute | solution.py:18
  492.7 6.2 %collective-permute-done.4 = bf16[384,128]{1,0:T(8,128)(2,1)} collective-permute-done((bf16[384,128]{1,0:T(8,128)(2,1)}, bf16[384,128]{1,0:T(8,128)(2,1)}, u32[]{:S(2)}, u32[]{:S(2)}) %collective-permute-start.4) | collective-permute-done | bytes 98336 | tf_op jit(solution)/shard_map/ppermute | solution.py:18
  498.9 7.2 %collective-permute-start.7 = (bf16[384,128]{1,0:T(8,128)(2,1)}, bf16[384,128]{1,0:T(8,128)(2,1)}, u32[]{:S(2)}, u32[]{:S(2)}) collective-permute-start(bf16[384,128]{1,0:T(8,128)(2,1)} %collective-permute-done.4), channel_id=1, source_target_pairs={{0,1},{1,2},{2,3},{4,5},{5,6},{6,7},{8,9},{9,10},{10,11},{12,13},{... | collective-permute-start | bytes 294920 | tf_op jit(solution)/shard_map/ppermute | solution.py:18
  506.1 2.6 convolution_add_fusion.3
  508.7 5.7 %conditional.3 = ((f32[4,384]{1,0:T(4,128)S(1)}, f32[4,384]{1,0:T(4,128)S(1)}, f32[4,384,128]{2,1,0:T(8,128)})) conditional(s32[]{:T(128)} %convert_element_type.53, (f32[4,384]{1,0:T(4,128)S(1)}, f32[4,384]{1,0:T(4,128)S(1)}, f32[4,384,128]{2,1,0:T(8,128)}) %tuple.31, (s32[]{:T(128)}, s32[384]{0:T(512)}, bf16[384]{0:T(512)(128)(2,1)}, ...), branch_computations={%region_2.3_spmd, %region_3.6_spmd} | conditional | flops 309611904 | bytes 16226396 | solution.py:106
  508.7 0.8 compare_and_fusion
  509.6 1.5 fusion.2
  511.1 0.5 fusion.1
  511.7 1.8 convolution_add_fusion
  513.5 0.9 copy-done.4
  514.4 0.0 collective-permute-done.6
  514.4 0.0 collective-permute-done.8
  514.4 0.0 collective-permute-done.7
  514.4 0.2 conditional.5
  514.6 1.4 fusion.49
  516.0 0.3 copy.10
  516.3 0.9 broadcast_in_dim_reshape.3
  (21 shorter events, 0.1 us)
Async XLA Ops:
  6.5 432.4 %copy-start = (bf16[1,384,4096]{2,1,0:T(8,128)(2,1)S(1)}, bf16[1,384,4096]{2,1,0:T(8,128)(2,1)}, u32[]{:S(2)}) copy-start(bf16[1,384,4096]{2,1,0:T(8,128)(2,1)} %param.9) | copy-start | bytes 9437188
  6.5 432.4 %all-gather.2.cloned.1.call-start = ((), (), s32[]{:S(2)}) async-start(), calls=%async_computation | async-start | bytes 6316032 | tf_op jit(solution)/shard_map/all_gather | solution.py:45
  8.2 436.2 %copy-start.10 = (bf16[384]{0:T(512)(128)(2,1)}, bf16[384]{0:T(512)(128)(2,1)S(1)}, u32[]{:S(2)}) copy-start(bf16[384]{0:T(512)(128)(2,1)S(1)} %convert_reduce_fusion) | copy-start | bytes 2308
  8.2 9.5 %collective-permute-start = (bf16[384]{0:T(512)(128)(2,1)S(1)}, bf16[384]{0:T(512)(128)(2,1)S(1)}, u32[]{:S(2)}, u32[]{:S(2)}) collective-permute-start(bf16[384]{0:T(512)(128)(2,1)S(1)} %convert_reduce_fusion), channel_id=1, source_target_pairs={{0,1},{1,2},{2,3},{4,5},{5,6},{6,7},{8,9},{9,10},{10,11},{12,13},{... | collective-permute-start | bytes 2312 | tf_op jit(solution)/shard_map/ppermute | solution.py:18
  16.4 427.9 %copy-start.9 = (s32[384]{0:T(512)}, s32[384]{0:T(512)S(1)}, u32[]{:S(2)}) copy-start(s32[384]{0:T(512)S(1)} %iota_add_fusion.3) | copy-start | bytes 4612
  17.7 426.7 %copy-start.11 = (bf16[384]{0:T(512)(128)(2,1)}, bf16[384]{0:T(512)(128)(2,1)S(1)}, u32[]{:S(2)}) copy-start(bf16[384]{0:T(512)(128)(2,1)S(1)} %collective-permute-done) | copy-start | bytes 2308
  17.7 9.5 %collective-permute-start.3 = (bf16[384]{0:T(512)(128)(2,1)S(1)}, bf16[384]{0:T(512)(128)(2,1)}, u32[]{:S(2)}, u32[]{:S(2)}) collective-permute-start(bf16[384]{0:T(512)(128)(2,1)S(1)} %collective-permute-done), channel_id=1, source_target_pairs={{0,1},{1,2},{2,3},{4,5},{5,6},{6,7},{8,9},{9,10},{10,11},{12,13},{... | collective-permute-start | bytes 2312 | tf_op jit(solution)/shard_map/ppermute | solution.py:18
  27.2 487.2 %collective-permute-start.6 = (bf16[384]{0:T(512)(128)(2,1)}, bf16[384]{0:T(512)(128)(2,1)}, u32[]{:S(2)}, u32[]{:S(2)}) collective-permute-start(bf16[384]{0:T(512)(128)(2,1)} %collective-permute-done.3), channel_id=1, source_target_pairs={{0,1},{1,2},{2,3},{4,5},{5,6},{6,7},{8,9},{9,10},{10,11},{12,13},{... | collective-permute-start | bytes 2312 | tf_op jit(solution)/shard_map/ppermute | solution.py:18
  444.4 7.0 %copy-start.1 = (f32[384,768]{1,0:T(8,128)}, f32[384,768]{1,0:T(8,128)S(1)}, u32[]{:S(2)}) copy-start(f32[384,768]{1,0:T(8,128)S(1)} %fusion.39) | copy-start | bytes 3538948
  446.1 21.2 %collective-permute-start.2 = (bf16[384,128]{1,0:T(8,128)(2,1)}, bf16[384,128]{1,0:T(8,128)(2,1)}, u32[]{:S(2)}, u32[]{:S(2)}) collective-permute-start(bf16[384,128]{1,0:T(8,128)(2,1)} %slice.39), channel_id=1, source_target_pairs={{0,1},{1,2},{2,3},{4,5},{5,6},{6,7},{8,9},{9,10},{10,11},{12,13},{... | collective-permute-start | bytes 294920 | tf_op jit(solution)/shard_map/ppermute | solution.py:18
  453.0 32.0 %collective-permute-start.1 = (bf16[384,128]{1,0:T(8,128)(2,1)}, bf16[384,128]{1,0:T(8,128)(2,1)}, u32[]{:S(2)}, u32[]{:S(2)}) collective-permute-start(bf16[384,128]{1,0:T(8,128)(2,1)} %pad_maximum_fusion.1), channel_id=1, source_target_pairs={{0,1},{1,2},{2,3},{4,5},{5,6},{6,7},{8,9},{9,10},{10,11},{12,13},{... | collective-permute-start | bytes 294920 | tf_op jit(solution)/shard_map/ppermute | solution.py:18
  460.2 0.9 copy-start.2
  467.3 19.8 %collective-permute-start.5 = (bf16[384,128]{1,0:T(8,128)(2,1)}, bf16[384,128]{1,0:T(8,128)(2,1)}, u32[]{:S(2)}, u32[]{:S(2)}) collective-permute-start(bf16[384,128]{1,0:T(8,128)(2,1)} %collective-permute-done.2), channel_id=1, source_target_pairs={{0,1},{1,2},{2,3},{4,5},{5,6},{6,7},{8,9},{9,10},{10,11},{12,13},{... | collective-permute-start | bytes 294920 | tf_op jit(solution)/shard_map/ppermute | solution.py:18
  484.9 14.0 %collective-permute-start.4 = (bf16[384,128]{1,0:T(8,128)(2,1)}, bf16[384,128]{1,0:T(8,128)(2,1)}, u32[]{:S(2)}, u32[]{:S(2)}) collective-permute-start(bf16[384,128]{1,0:T(8,128)(2,1)} %collective-permute-done.1), channel_id=1, source_target_pairs={{0,1},{1,2},{2,3},{4,5},{5,6},{6,7},{8,9},{9,10},{10,11},{12,13},{... | collective-permute-start | bytes 294920 | tf_op jit(solution)/shard_map/ppermute | solution.py:18
  487.0 27.4 %collective-permute-start.8 = (bf16[384,128]{1,0:T(8,128)(2,1)}, bf16[384,128]{1,0:T(8,128)(2,1)}, u32[]{:S(2)}, u32[]{:S(2)}) collective-permute-start(bf16[384,128]{1,0:T(8,128)(2,1)} %collective-permute-done.5), channel_id=1, source_target_pairs={{0,1},{1,2},{2,3},{4,5},{5,6},{6,7},{8,9},{9,10},{10,11},{12,13},{... | collective-permute-start | bytes 294920 | tf_op jit(solution)/shard_map/ppermute | solution.py:18
  498.9 15.5 %collective-permute-start.7 = (bf16[384,128]{1,0:T(8,128)(2,1)}, bf16[384,128]{1,0:T(8,128)(2,1)}, u32[]{:S(2)}, u32[]{:S(2)}) collective-permute-start(bf16[384,128]{1,0:T(8,128)(2,1)} %collective-permute-done.4), channel_id=1, source_target_pairs={{0,1},{1,2},{2,3},{4,5},{5,6},{6,7},{8,9},{9,10},{10,11},{12,13},{... | collective-permute-start | bytes 294920 | tf_op jit(solution)/shard_map/ppermute | solution.py:18
  509.6 2.1 copy-start.3
  513.5 0.9 copy-start.4
Sparse Core Ops, SparseCore 0:
  10.1 428.8 all-gather.1
where the time goes:
time: 525 us; the launch traced here: 524 us
  waiting for transfers between devices  431 us (82%)
  starting transfers between devices  51.3 us (10%)
  between operations  13.6 us (3%)
  matrix products  12.7 us (2%)
  local copies, waits for them, and re-layouts  8.37 us (2%)
  other arithmetic  7.12 us (1%)
    all_gather x1, waiting for transfers between devices, body(): lax.all_gather(qkv_weight, 'fsdp', axis=0, tiled=True)  404 us
    ppermute x9, starting transfers between devices, shifted(): lax.ppermute(value, axis, [(source, source + steps) for source in range(f...  51.3 us
    ppermute x9, waiting for transfers between devices, shifted(): lax.ppermute(value, axis, [(source, source + steps) for source in range(f...  26.3 us
  transfers between devices with their start and end apart: 10, of which 7 were waited for; matrix products, arithmetic and copies ran while one was open for 5% of the time, Pallas kernels for 0%

commit v1 on v0

v1 whole, which is shorter than its diff:
```python
import functools
import math

import jax
import jax.numpy as jnp
from jax import lax
from jax.experimental import pallas as pl
from jax.experimental.pallas import tpu as pltpu
from jax.sharding import PartitionSpec as P

MESH = pl.DeviceIdType.MESH
HEADS = 4
HD = 128
THETA = 1000000.0
X, ZL, Y, ZH = 4, 4, 8, 4
Z = ZL * ZH
SCALE2 = math.log2(math.e) / math.sqrt(HD)


def kernel(hid, w_in, doc, out, wbuf, hbuf, kv, docs, qs, acc, m_s, l_s, bias, cos_s, sin_s,
           loc_sem, zs, zr, rs, rr, ss, sr, kvs, kvr, ds, dr):
    rows = hid.shape[1]
    shard = w_in.shape[0]
    depth = X * ZL * Y * 2 * shard
    f = lax.axis_index("fsdp")
    ctx = lax.axis_index("ctx")
    core = lax.rem(f, 2)
    y = lax.rem(f // 2, Y)
    zl = lax.rem(f // (2 * Y), ZL)
    x = f // (2 * Y * ZL)
    z = ctx * ZL + zl

    def device(x_, z_, y_, core_):
        return {"fsdp": ((x_ * ZL + lax.rem(z_, ZL)) * Y + y_) * 2 + core_, "ctx": z_ // ZL}

    def shift(v, d, n):
        return lax.rem(v + d + n, n)

    z_peers = [shift(z, 1, Z), shift(z, -1, Z), shift(z, 2, Z)]
    sibling = device(x, z, y, 1 - core)
    x_right, x_left = device(shift(x, 1, X), z, y, core), device(shift(x, -1, X), z, y, core)
    y_right, y_left = device(x, z, shift(y, 1, Y), core), device(x, z, shift(y, -1, Y), core)
    ctx_right = {"fsdp": f, "ctx": shift(ctx, 1, ZH)}
    ctx_left = {"fsdp": f, "ctx": shift(ctx, -1, ZH)}

    def remote(src, dst, send, recv, dev):
        return pltpu.make_async_remote_copy(
            src_ref=src, dst_ref=dst, send_sem=send, recv_sem=recv, device_id=dev,
            device_id_type=MESH,
        )

    barrier = pltpu.get_barrier_semaphore()
    peers = [sibling, x_right, x_left, y_right, y_left, ctx_right, ctx_left]
    for z_ in z_peers + [shift(z, -2, Z)]:
        peers += [device(x, z_, y, 0), device(x, z_, y, 1)]
    hid_copy = pltpu.make_async_copy(hid.at[0], hbuf, loc_sem.at[0])
    hid_copy.start()
    for dev in peers:
        pl.semaphore_signal(barrier, inc=1, device_id=dev, device_id_type=MESH)
    pl.semaphore_wait(barrier, len(peers))

    def column(j, cc):
        start = (HEADS + cc) * HD if j == 0 else ((j - 1) * 2 + cc) * HD
        return pl.ds(pl.multiple_of(start, HD), HD)

    def z_slot(j, cc, zl_, core_):
        return wbuf.at[j, cc, x, zl_, y, pl.ds(pl.multiple_of(core_ * shard, shard), shard)]

    def z_send(j, k):
        cc = 1 - core if k % 2 else core
        if k < 2:
            dev = sibling
        else:
            dev = device(x, z_peers[k // 2 - 1], y, cc)
        return remote(
            w_in.at[:, column(j, cc)], z_slot(j, cc, zl, core), zs.at[j, k], zr.at[j, k], dev
        )

    def z_own(j):
        return pltpu.make_async_copy(
            w_in.at[:, column(j, core)], z_slot(j, core, zl, core), zr.at[j, 0]
        )

    def z_wait(j):
        z_own(j).wait()
        for k in range(1, 8):
            from_core = 1 - core if k % 2 else core
            from_zl = lax.rem(zl + (0, -1, 1, -2)[k // 2] + ZL, ZL)
            slot = z_slot(j, core, from_zl, from_core)
            remote(slot, slot, zs.at[j, k], zr.at[j, k], sibling).wait_recv()

    for j in range(3):
        z_own(j).start()
        for k in (7, 6, 5, 4, 3, 2, 1):
            z_send(j, k).start()

    doc_right = remote(doc, docs.at[ctx], ds.at[0], dr.at[ctx], ctx_right)
    doc_left = remote(doc, docs.at[ctx], ds.at[1], dr.at[ctx], ctx_left)
    before = jnp.maximum(ctx - 1, 0)
    doc_relay = remote(docs.at[before], docs.at[before], ds.at[2], dr.at[before], ctx_right)

    @pl.when(ctx < ZH - 1)
    def _():
        doc_right.start()

    @pl.when(ctx == 0)
    def _():
        doc_left.start()

    lane = lax.broadcasted_iota(jnp.int32, (1, HD), 1)
    half_lane = jnp.where(lane < HD // 2, lane, lane - HD // 2).astype(jnp.float32)
    frequency = jnp.exp(half_lane * (-2.0 * math.log(THETA) / HD))
    position = (ctx * rows + lax.broadcasted_iota(jnp.int32, (rows, 1), 0)).astype(jnp.float32)
    angles = position * frequency
    cos_s[...] = jnp.cos(angles)
    sin_s[...] = jnp.sin(angles) * jnp.where(lane < HD // 2, -1.0, 1.0)

    def rotary(v):
        return (v * cos_s[...] + pltpu.roll(v, HD // 2, 1) * sin_s[...]).astype(jnp.bfloat16)

    def block(stage, cc, js, i, half=None):
        zz = slice(None) if half is None else slice(half * (ZL // 2), (half + 1) * (ZL // 2))
        along_x = (stage == 0) == (cc == 1)
        if along_x:
            if stage == 0:
                return wbuf.at[js, cc, i, zz, y]
            return wbuf.at[js, cc, i, zz]
        if stage == 0:
            return wbuf.at[js, cc, x, zz, i]
        return wbuf.at[js, cc, :, zz, i]

    class Ring:
        def __init__(self, phase, stage, cc):
            self.phase, self.stage, self.cc = phase, stage, cc
            self.js = slice(0, 1) if phase == 0 else slice(1, 3)
            along_x = (stage == 0) == (cc == 1)
            self.n = X if along_x else Y
            self.p = x if along_x else y
            self.dev = (x_right, x_left) if along_x else (y_right, y_left)
            self.steps = self.n // 2

        def received(self, d, s):
            half = d if s == self.steps else None
            return block(self.stage, self.cc, self.js,
                         shift(self.p, -s if d == 0 else s, self.n), half)

        def copy(self, d, s):
            half = d if s == self.steps else None
            i = shift(self.p, 1 - s if d == 0 else s - 1, self.n)
            ref = block(self.stage, self.cc, self.js, i, half)
            at = (self.phase, self.stage, d, s - 1)
            return remote(ref, ref, rs.at[at], rr.at[at], self.dev[d])

        def start(self, s):
            for d in range(2):
                self.copy(d, s).start()

        def wait(self, s, d):
            ref = self.received(d, s)
            at = (self.phase, self.stage, d, s - 1)
            remote(ref, ref, rs.at[at], rr.at[at], self.dev[d]).wait_recv()

        def done(self):
            for s in range(1, self.steps + 1):
                for d in range(2):
                    self.copy(d, s).wait_send()

        def pieces(self):
            own = [block(self.stage, self.cc, self.js, self.p)]
            return own + [self.received(d, s) for s in range(1, self.steps + 1) for d in range(2)]

    def forward(ring, k):
        ref = ring.pieces()[k]
        at = (ring.phase, k)
        return remote(ref, ref, ss.at[at], sr.at[at], sibling)

    def last_stage(ring):
        ring.start(1)
        forward(ring, 0).start()
        for s in range(1, ring.steps + 1):
            for d in range(2):
                ring.wait(s, d)
                if s < ring.steps:
                    ring.copy(d, s + 1).start()
            for d in range(2):
                forward(ring, 1 + (s - 1) * 2 + d).start()

    def n_pieces(ring):
        return 1 + 2 * ring.steps

    def project(j, groups):
        chunk = depth // X

        def step(i, total):
            w = jnp.concatenate(
                [wbuf[j, cc, i].reshape(chunk, HD) for cc in groups], axis=1
            ) if len(groups) > 1 else wbuf[j, groups[0], i].reshape(chunk, HD)
            h = hbuf[:, pl.ds(pl.multiple_of(i * chunk, chunk), chunk)]
            return total + jnp.dot(h, w, preferred_element_type=jnp.float32)

        return lax.fori_loop(0, X, step, jnp.zeros((rows, HD * len(groups)), jnp.float32))

    def kv_copy(kind, way):
        if way == 0:
            return remote(kv.at[kind, ctx], kv.at[kind, ctx], kvs.at[kind, 0],
                          kvr.at[kind, ctx], ctx_right)
        if way == 1:
            return remote(kv.at[kind, ctx], kv.at[kind, ctx], kvs.at[kind, 1],
                          kvr.at[kind, ctx], ctx_left)
        b = before if kind == 0 else jnp.where(ctx == 0, 1, 0)
        dev = ctx_right if kind == 0 else ctx_left
        return remote(kv.at[kind, b], kv.at[kind, b], kvs.at[kind, 2], kvr.at[kind, b], dev)

    def kv_sends(kind, act):
        left = ctx == 0 if kind == 0 else ctx <= 1

        @pl.when(left)
        def _():
            act(kv_copy(kind, 1))

        @pl.when(ctx < ZH - 1)
        def _():
            act(kv_copy(kind, 0))

    def make(kind):
        if kind == 0:
            kv[0, ctx] = rotary(project(0, (0,)))
        else:
            kv[1, ctx] = project(0, (1,)).astype(jnp.bfloat16)
        kv_sends(kind, lambda c: c.start())

    for cc in range(2):

        @pl.when(core == cc)
        def _():
            kv1, kv2, q1, q2 = Ring(0, 0, cc), Ring(0, 1, cc), Ring(1, 0, cc), Ring(1, 1, cc)
            other1, other2 = Ring(0, 1, 1 - cc), Ring(1, 1, 1 - cc)
            z_wait(0)
            kv1.start(1)
            z_wait(1)
            z_wait(2)
            q1.start(1)
            for s in range(1, kv1.steps + 1):
                for ring in (kv1, q1):
                    for d in range(2):
                        ring.wait(s, d)
                        if s < ring.steps:
                            ring.copy(d, s + 1).start()
            last_stage(kv2)
            hid_copy.wait()
            make(cc)
            for k in range(n_pieces(other1)):
                forward(other1, k).wait_recv()
            make(1 - cc)
            last_stage(q2)
            for k in range(n_pieces(other2)):
                forward(other2, k).wait_recv()
            for ring in (kv1, kv2, q1, q2):
                ring.done()
            for ring in (kv2, q2):
                for k in range(n_pieces(ring)):
                    forward(ring, k).wait_send()

    for j in range(3):
        for k in range(1, 8):
            z_send(j, k).wait_send()

    def arrived(kind, b):
        remote(kv.at[kind, b], kv.at[kind, b], kvs.at[kind, 0], kvr.at[kind, b],
               ctx_right).wait_recv()

    def docs_arrived(b):
        remote(docs.at[b], docs.at[b], ds.at[0], dr.at[b], ctx_right).wait_recv()

    @pl.when((ctx == 1) | (ctx == 2))
    def _():
        docs_arrived(before)
        doc_relay.start()
        arrived(0, before)
        kv_copy(0, 2).start()

    @pl.when((ctx == 0) | (ctx == 3))
    def _():
        arrived(1, jnp.where(ctx == 0, 1, 0))
        kv_copy(1, 2).start()

    for j in range(2):
        pair = project(1 + j, (0, 1))
        for i in range(2):
            qs[2 * j + i] = rotary(pair[:, i * HD : (i + 1) * HD])

    token = lax.broadcasted_iota(jnp.int32, (rows, 1), 0)
    zeros_here = jnp.sum(jnp.where(doc[...] == 0, 1.0, 0.0), axis=1, keepdims=True)
    doc_query = jnp.where(token.astype(jnp.float32) >= zeros_here, 1.0, 0.0)

    def scores(h, b):
        s = lax.dot_general(
            qs[h], kv[0, b], (((1,), (1,)), ((), ())), preferred_element_type=jnp.float32
        )
        return s * SCALE2 + bias[...]

    same = doc_query == doc[...].astype(jnp.float32)
    causal = lax.broadcasted_iota(jnp.int32, (rows, rows), 1) <= token
    bias[...] = jnp.where(same & causal, 0.0, -jnp.inf)

    def first(h, _):
        s = scores(h, ctx)
        top = jnp.max(s, axis=1, keepdims=True)
        p = jnp.exp2(s - top)
        m_s[h] = top
        l_s[h] = jnp.sum(p, axis=1, keepdims=True)
        acc[h] = jnp.dot(p.astype(jnp.bfloat16), kv[1, ctx], preferred_element_type=jnp.float32)
        return 0

    lax.fori_loop(0, HEADS, first, 0)

    def later(t, _):
        b = jnp.where(t == 0, ctx - 1, t - 1)

        @pl.when(jnp.logical_not(((ctx == 1) | (ctx == 2)) & (b == ctx - 1)))
        def _():
            docs_arrived(b)
            arrived(0, b)

        @pl.when(jnp.logical_not((ctx == 3) & (b == 0)))
        def _():
            arrived(1, b)

        bias[...] = jnp.where(doc_query == docs[b].astype(jnp.float32), 0.0, -jnp.inf)

        def update(h, _):
            s = scores(h, b)
            old = m_s[h]
            top = jnp.maximum(old, jnp.max(s, axis=1, keepdims=True))
            p = jnp.exp2(s - top)
            factor = jnp.exp2(old - top)
            m_s[h] = top
            l_s[h] = l_s[h] * factor + jnp.sum(p, axis=1, keepdims=True)
            acc[h] = acc[h] * factor + jnp.dot(
                p.astype(jnp.bfloat16), kv[1, b], preferred_element_type=jnp.float32
            )
            return 0

        lax.fori_loop(0, HEADS, update, 0)
        return 0

    lax.fori_loop(0, ctx, later, 0)

    for h in range(HEADS):
        out[:, h * HD : (h + 1) * HD] = (acc[h] / l_s[h]).astype(jnp.bfloat16)

    for kind in range(2):
        kv_sends(kind, lambda c: c.wait_send())

    @pl.when(ctx < ZH - 1)
    def _():
        doc_right.wait_send()

    @pl.when(ctx == 0)
    def _():
        doc_left.wait_send()

    @pl.when((ctx == 1) | (ctx == 2))
    def _():
        doc_relay.wait_send()
        kv_copy(0, 2).wait_send()

    @pl.when((ctx == 0) | (ctx == 3))
    def _():
        kv_copy(1, 2).wait_send()


def body(hidden_states, qkv_weight, doc_ids):
    rows, width = hidden_states.shape[1:]
    shard = qkv_weight.shape[0]
    dma = pltpu.SemaphoreType.DMA
    steps = max(X, Y) // 2
    result = pl.pallas_call(
        kernel,
        out_shape=jax.ShapeDtypeStruct((rows, HEADS * HD), jnp.bfloat16),
        in_specs=[
            pl.BlockSpec(memory_space=pl.ANY),
            pl.BlockSpec(memory_space=pl.ANY),
            pl.BlockSpec(memory_space=pltpu.VMEM),
        ],
        out_specs=pl.BlockSpec(memory_space=pltpu.VMEM),
        scratch_shapes=[
            pltpu.VMEM((3, 2, X, ZL, Y, 2 * shard, HD), jnp.bfloat16),
            pltpu.VMEM((rows, width), jnp.bfloat16),
            pltpu.VMEM((2, ZH, rows, HD), jnp.bfloat16),
            pltpu.VMEM((ZH, 1, rows), jnp.int32),
            pltpu.VMEM((HEADS, rows, HD), jnp.bfloat16),
            pltpu.VMEM((HEADS, rows, HD), jnp.float32),
            pltpu.VMEM((HEADS, rows, 1), jnp.float32),
            pltpu.VMEM((HEADS, rows, 1), jnp.float32),
            pltpu.VMEM((rows, rows), jnp.float32),
            pltpu.VMEM((rows, HD), jnp.float32),
            pltpu.VMEM((rows, HD), jnp.float32),
            dma((1,)),
            dma((3, 8)),
            dma((3, 8)),
            dma((2, 2, 2, steps)),
            dma((2, 2, 2, steps)),
            dma((2, 2 * steps + 1)),
            dma((2, 2 * steps + 1)),
            dma((2, 3)),
            dma((2, ZH)),
            dma((3,)),
            dma((ZH,)),
        ],
        compiler_params=pltpu.CompilerParams(
            collective_id=0, has_side_effects=True, vmem_limit_bytes=60 * 1024 * 1024
        ),
    )(hidden_states, qkv_weight, doc_ids)
    return result[None]


def solution(mesh):
    in_specs = (P("fsdp", "ctx", None), P("fsdp", None), P("fsdp", "ctx"))
    out_specs = P("fsdp", "ctx", None)
    return jax.shard_map(body, mesh=mesh, in_specs=in_specs, out_specs=out_specs, check_vma=False)
```

time: 525 us -> 85.7 us (0.16)
  the two profiles are of different devices: /device:TPU:448 before, /device:TPU:1 now
where the time goes in v1:
time: 85.7 us; the launch traced here: 85.5 us
  Pallas kernels  83.7 us (98%)
  local copies, waits for them, and re-layouts  1.77 us (2%)
    pallas_call x1, Pallas kernels, body(): pl.pallas_call(kernel, out_shape=jax.ShapeDtypeStruct((rows, HEADS * HD),...  83.7 us
    unnamed x1, local copies, waits for them, and re-layouts  1.77 us

profile of v1, /device:TPU:1, one launch (start us, length us, event | category | flops | bytes accessed | tf_op | source)
XLA Modules:
  0.0 85.5 jit_solution(9052939448209199515)
XLA Ops:
  0.0 83.7 %shard_map.37 = bf16[384,512]{1,0:T(8,128)(2,1)} custom-call(bf16[1,384,4096]{2,1,0:T(8,128)(2,1)} %hid.1, bf16[16,768]{1,0:T(8,128)(2,1)} %w_in.1, s32[1,384]{1,0:T(1,128)} %doc.1), custom_call_target="tpu_custom_call" | custom-call | tf_op jit(solution)/shard_map/pallas_call | solution.py:378
  83.7 1.8 %copy.5 = bf16[1,384,512]{2,1,0:T(8,128)(2,1)} copy(bf16[1,384,512]{2,1,0:T(8,128)(2,1)} %bitcast.1) | data formatting | bytes 786432

commit v2 on v1

--- a/solution.py
+++ b/solution.py
@@ -18,7 +18,7 @@
 
 
 def kernel(hid, w_in, doc, out, wbuf, hbuf, kv, docs, qs, acc, m_s, l_s, bias, cos_s, sin_s,
-           loc_sem, zs, zr, rs, rr, ss, sr, kvs, kvr, ds, dr):
+           loc_sem, zs, zr, s1, r1, s2, r2, ss, sr, kvs, kvr, ds, dr):
     rows = hid.shape[1]
     shard = w_in.shape[0]
     depth = X * ZL * Y * 2 * shard
@@ -50,7 +50,9 @@
         )
 
     barrier = pltpu.get_barrier_semaphore()
-    peers = [sibling, x_right, x_left, y_right, y_left, ctx_right, ctx_left]
+    peers = [ctx_right, ctx_left, sibling]
+    peers += [device(shift(x, d, X), z, y, core) for d in range(1, X)]
+    peers += [device(x, z, shift(y, d, Y), core) for d in range(1, Y)]
     for z_ in z_peers + [shift(z, -2, Z)]:
         peers += [device(x, z_, y, 0), device(x, z_, y, 1)]
     hid_copy = pltpu.make_async_copy(hid.at[0], hbuf, loc_sem.at[0])
@@ -118,75 +120,98 @@
     def rotary(v):
         return (v * cos_s[...] + pltpu.roll(v, HD // 2, 1) * sin_s[...]).astype(jnp.bfloat16)
 
-    def block(stage, cc, js, i, half=None):
-        zz = slice(None) if half is None else slice(half * (ZL // 2), (half + 1) * (ZL // 2))
-        along_x = (stage == 0) == (cc == 1)
-        if along_x:
-            if stage == 0:
-                return wbuf.at[js, cc, i, zz, y]
-            return wbuf.at[js, cc, i, zz]
-        if stage == 0:
-            return wbuf.at[js, cc, x, zz, i]
-        return wbuf.at[js, cc, :, zz, i]
-
-    class Ring:
-        def __init__(self, phase, stage, cc):
-            self.phase, self.stage, self.cc = phase, stage, cc
+    class Gather:
+        def __init__(self, phase, cc):
+            self.phase, self.cc = phase, cc
             self.js = slice(0, 1) if phase == 0 else slice(1, 3)
-            along_x = (stage == 0) == (cc == 1)
-            self.n = X if along_x else Y
-            self.p = x if along_x else y
-            self.dev = (x_right, x_left) if along_x else (y_right, y_left)
-            self.steps = self.n // 2
-
-        def received(self, d, s):
+            self.n1, self.p1 = (Y, y) if cc == 0 else (X, x)
+            self.n2, self.p2 = (X, x) if cc == 0 else (Y, y)
+            self.dev = (x_right, x_left) if cc == 0 else (y_right, y_left)
+            self.steps = self.n2 // 2
+
+        def piece(self, i, q, half=None):
+            zz = slice(None) if half is None else slice(half * (ZL // 2), (half + 1) * (ZL // 2))
+            if self.cc == 0:
+                return wbuf.at[self.js, 0, q, zz, i]
+            return wbuf.at[self.js, 1, i, zz, q]
+
+        def offset(self, k):
+            return (k + 1) // 2 * (1 - 2 * lax.rem(k + 1, 2))
+
+        def direct(self, k):
+            ref = self.piece(self.p1, self.p2)
+            to = lax.rem(self.p1 + self.offset(k) + self.n1, self.n1)
+            dev = device(x, z, to, core) if self.cc == 0 else device(to, z, y, core)
+            return remote(ref, ref, s1.at[self.phase, k], r1.at[self.phase, k], dev)
+
+        def index(self, k):
+            return lax.rem(self.p1 - self.offset(k) + self.n1, self.n1)
+
+        def at(self, d, s, k):
             half = d if s == self.steps else None
-            return block(self.stage, self.cc, self.js,
-                         shift(self.p, -s if d == 0 else s, self.n), half)
-
-        def copy(self, d, s):
+            return self.piece(self.index(k), shift(self.p2, -s if d == 0 else s, self.n2), half)
+
+        def copy(self, d, s, k):
             half = d if s == self.steps else None
-            i = shift(self.p, 1 - s if d == 0 else s - 1, self.n)
-            ref = block(self.stage, self.cc, self.js, i, half)
-            at = (self.phase, self.stage, d, s - 1)
-            return remote(ref, ref, rs.at[at], rr.at[at], self.dev[d])
-
-        def start(self, s):
+            ref = self.piece(self.index(k), shift(self.p2, 1 - s if d == 0 else s - 1, self.n2), half)
+            return remote(ref, ref, s2.at[self.phase, d], r2.at[self.phase, d, s - 1, k], self.dev[d])
+
+        def forward(self, ref):
+            return remote(ref, ref, ss.at[self.phase], sr.at[self.phase], sibling)
+
+        def start(self):
+            def step(k, _):
+                self.direct(k).start()
+                return 0
+
+            lax.fori_loop(1, self.n1, step, 0)
+
+        def own(self):
+            def step(k, _):
+                ref = self.piece(self.index(k), self.p2)
+
+                @pl.when(k > 0)
+                def _():
+                    remote(ref, ref, s1.at[self.phase, k], r1.at[self.phase, k], sibling).wait_recv()
+
+                for d in range(2):
+                    self.copy(d, 1, k).start()
+                self.forward(ref).start()
+                return 0
+
+            lax.fori_loop(0, self.n1, step, 0)
+
+        def relay(self, s):
+            def step(k, _):
+                for d in range(2):
+                    ref = self.at(d, s, k)
+                    remote(ref, ref, s2.at[self.phase, d], r2.at[self.phase, d, s - 1, k],
+                           self.dev[d]).wait_recv()
+                    if s < self.steps:
+                        self.copy(d, s + 1, k).start()
+                    self.forward(ref).start()
+                return 0
+
+            lax.fori_loop(0, self.n1, step, 0)
+
+        def sibling_done(self):
+            ref = wbuf.at[self.js, 1 - self.cc]
+            remote(ref, ref, ss.at[self.phase], sr.at[self.phase], sibling).wait_recv()
+
+        def done(self):
+            def step(k, _):
+                self.direct(k).wait_send()
+                return 0
+
+            lax.fori_loop(1, self.n1, step, 0)
+            if self.cc == 0:
+                sent = wbuf.at[self.js, 0, 0 : X - 1, :, 0 : Y // 2]
+            else:
+                sent = wbuf.at[self.js, 1, :, 0 : ZL // 2, 0 : Y - 1]
             for d in range(2):
-                self.copy(d, s).start()
-
-        def wait(self, s, d):
-            ref = self.received(d, s)
-            at = (self.phase, self.stage, d, s - 1)
-            remote(ref, ref, rs.at[at], rr.at[at], self.dev[d]).wait_recv()
-
-        def done(self):
-            for s in range(1, self.steps + 1):
-                for d in range(2):
-                    self.copy(d, s).wait_send()
-
-        def pieces(self):
-            own = [block(self.stage, self.cc, self.js, self.p)]
-            return own + [self.received(d, s) for s in range(1, self.steps + 1) for d in range(2)]
-
-    def forward(ring, k):
-        ref = ring.pieces()[k]
-        at = (ring.phase, k)
-        return remote(ref, ref, ss.at[at], sr.at[at], sibling)
-
-    def last_stage(ring):
-        ring.start(1)
-        forward(ring, 0).start()
-        for s in range(1, ring.steps + 1):
-            for d in range(2):
-                ring.wait(s, d)
-                if s < ring.steps:
-                    ring.copy(d, s + 1).start()
-            for d in range(2):
-                forward(ring, 1 + (s - 1) * 2 + d).start()
-
-    def n_pieces(ring):
-        return 1 + 2 * ring.steps
+                remote(sent, sent, s2.at[self.phase, d], r2.at[self.phase, d, 0, 0],
+                       self.dev[d]).wait_send()
+            self.forward(wbuf.at[self.js, self.cc]).wait_send()
 
     def project(j, groups):
         chunk = depth // X
@@ -229,60 +254,55 @@
             kv[1, ctx] = project(0, (1,)).astype(jnp.bfloat16)
         kv_sends(kind, lambda c: c.start())
 
+    def arrived(kind, b):
+        remote(kv.at[kind, b], kv.at[kind, b], kvs.at[kind, 0], kvr.at[kind, b],
+               ctx_right).wait_recv()
+
+    def docs_arrived(b):
+        remote(docs.at[b], docs.at[b], ds.at[0], dr.at[b], ctx_right).wait_recv()
+
+    def relays():
+        @pl.when((ctx == 1) | (ctx == 2))
+        def _():
+            docs_arrived(before)
+            doc_relay.start()
+            arrived(0, before)
+            kv_copy(0, 2).start()
+
+        @pl.when((ctx == 0) | (ctx == 3))
+        def _():
+            arrived(1, jnp.where(ctx == 0, 1, 0))
+            kv_copy(1, 2).start()
+
     for cc in range(2):
 
         @pl.when(core == cc)
         def _():
-            kv1, kv2, q1, q2 = Ring(0, 0, cc), Ring(0, 1, cc), Ring(1, 0, cc), Ring(1, 1, cc)
-            other1, other2 = Ring(0, 1, 1 - cc), Ring(1, 1, 1 - cc)
+            now, later_on = Gather(0, cc), Gather(1, cc)
             z_wait(0)
-            kv1.start(1)
+            now.start()
+            now.own()
+            for s in range(1, now.steps + 1):
+                now.relay(s)
             z_wait(1)
             z_wait(2)
-            q1.start(1)
-            for s in range(1, kv1.steps + 1):
-                for ring in (kv1, q1):
-                    for d in range(2):
-                        ring.wait(s, d)
-                        if s < ring.steps:
-                            ring.copy(d, s + 1).start()
-            last_stage(kv2)
+            later_on.start()
             hid_copy.wait()
             make(cc)
-            for k in range(n_pieces(other1)):
-                forward(other1, k).wait_recv()
+            now.sibling_done()
             make(1 - cc)
-            last_stage(q2)
-            for k in range(n_pieces(other2)):
-                forward(other2, k).wait_recv()
-            for ring in (kv1, kv2, q1, q2):
-                ring.done()
-            for ring in (kv2, q2):
-                for k in range(n_pieces(ring)):
-                    forward(ring, k).wait_send()
+            later_on.own()
+            for s in range(1, later_on.steps + 1):
+                if s == later_on.steps:
+                    relays()
+                later_on.relay(s)
+            later_on.sibling_done()
+            now.done()
+            later_on.done()
 
     for j in range(3):
         for k in range(1, 8):
             z_send(j, k).wait_send()
-
-    def arrived(kind, b):
-        remote(kv.at[kind, b], kv.at[kind, b], kvs.at[kind, 0], kvr.at[kind, b],
-               ctx_right).wait_recv()
-
-    def docs_arrived(b):
-        remote(docs.at[b], docs.at[b], ds.at[0], dr.at[b], ctx_right).wait_recv()
-
-    @pl.when((ctx == 1) | (ctx == 2))
-    def _():
-        docs_arrived(before)
-        doc_relay.start()
-        arrived(0, before)
-        kv_copy(0, 2).start()
-
-    @pl.when((ctx == 0) | (ctx == 3))
-    def _():
-        arrived(1, jnp.where(ctx == 0, 1, 0))
-        kv_copy(1, 2).start()
 
     for j in range(2):
         pair = project(1 + j, (0, 1))
@@ -399,10 +419,12 @@
             dma((1,)),
             dma((3, 8)),
             dma((3, 8)),
-            dma((2, 2, 2, steps)),
-            dma((2, 2, 2, steps)),
-            dma((2, 2 * steps + 1)),
-            dma((2, 2 * steps + 1)),
+            dma((2, Y)),
+            dma((2, Y)),
+            dma((2, 2)),
+            dma((2, 2, steps, Y)),
+            dma((2,)),
+            dma((2,)),
             dma((2, 3)),
             dma((2, ZH)),
             dma((3,)),

time: 85.7 us -> 78.2 us (0.912)
  the two profiles are of different devices: /device:TPU:1 before, /device:TPU:769 now
where the time goes in v2:
time: 78.2 us; the launch traced here: 78 us
  Pallas kernels  76.2 us (97%)
  local copies, waits for them, and re-layouts  1.77 us (2%)
    pallas_call x1, Pallas kernels, body(): pl.pallas_call(kernel, out_shape=jax.ShapeDtypeStruct((rows, HEADS * HD),...  76.2 us
    unnamed x1, local copies, waits for them, and re-layouts  1.77 us

profile of v2, /device:TPU:769, one launch (start us, length us, event | category | flops | bytes accessed | tf_op | source)
XLA Modules:
  0.0 78.0 jit_solution(7007896733028074826)
XLA Ops:
  0.0 76.2 %shard_map.37 = bf16[384,512]{1,0:T(8,128)(2,1)} custom-call(bf16[1,384,4096]{2,1,0:T(8,128)(2,1)} %hid.1, bf16[16,768]{1,0:T(8,128)(2,1)} %w_in.1, s32[1,384]{1,0:T(1,128)} %doc.1), custom_call_target="tpu_custom_call" | custom-call | tf_op jit(solution)/shard_map/pallas_call | solution.py:398
  76.2 1.8 %copy.5 = bf16[1,384,512]{2,1,0:T(8,128)(2,1)} copy(bf16[1,384,512]{2,1,0:T(8,128)(2,1)} %bitcast.1) | data formatting | bytes 786432

commit v3 on v2

--- a/solution.py
+++ b/solution.py
@@ -91,31 +91,37 @@
             slot = z_slot(j, core, from_zl, from_core)
             remote(slot, slot, zs.at[j, k], zr.at[j, k], sibling).wait_recv()
 
-    for j in range(3):
-        z_own(j).start()
+    def z_start(j):
         for k in (7, 6, 5, 4, 3, 2, 1):
             z_send(j, k).start()
+        z_own(j).start()
+
+    z_start(0)
 
     doc_right = remote(doc, docs.at[ctx], ds.at[0], dr.at[ctx], ctx_right)
     doc_left = remote(doc, docs.at[ctx], ds.at[1], dr.at[ctx], ctx_left)
     before = jnp.maximum(ctx - 1, 0)
     doc_relay = remote(docs.at[before], docs.at[before], ds.at[2], dr.at[before], ctx_right)
 
-    @pl.when(ctx < ZH - 1)
-    def _():
-        doc_right.start()
-
-    @pl.when(ctx == 0)
-    def _():
-        doc_left.start()
-
-    lane = lax.broadcasted_iota(jnp.int32, (1, HD), 1)
-    half_lane = jnp.where(lane < HD // 2, lane, lane - HD // 2).astype(jnp.float32)
-    frequency = jnp.exp(half_lane * (-2.0 * math.log(THETA) / HD))
-    position = (ctx * rows + lax.broadcasted_iota(jnp.int32, (rows, 1), 0)).astype(jnp.float32)
-    angles = position * frequency
-    cos_s[...] = jnp.cos(angles)
-    sin_s[...] = jnp.sin(angles) * jnp.where(lane < HD // 2, -1.0, 1.0)
+    def aside():
+        @pl.when(ctx < ZH - 1)
+        def _():
+            doc_right.start()
+
+        @pl.when(ctx == 0)
+        def _():
+            doc_left.start()
+
+        z_start(1)
+        z_start(2)
+
+        lane = lax.broadcasted_iota(jnp.int32, (1, HD), 1)
+        half_lane = jnp.where(lane < HD // 2, lane, lane - HD // 2).astype(jnp.float32)
+        frequency = jnp.exp(half_lane * (-2.0 * math.log(THETA) / HD))
+        position = (ctx * rows + lax.broadcasted_iota(jnp.int32, (rows, 1), 0)).astype(jnp.float32)
+        angles = position * frequency
+        cos_s[...] = jnp.cos(angles)
+        sin_s[...] = jnp.sin(angles) * jnp.where(lane < HD // 2, -1.0, 1.0)
 
     def rotary(v):
         return (v * cos_s[...] + pltpu.roll(v, HD // 2, 1) * sin_s[...]).astype(jnp.bfloat16)
@@ -225,34 +231,40 @@
 
         return lax.fori_loop(0, X, step, jnp.zeros((rows, HD * len(groups)), jnp.float32))
 
-    def kv_copy(kind, way):
-        if way == 0:
-            return remote(kv.at[kind, ctx], kv.at[kind, ctx], kvs.at[kind, 0],
-                          kvr.at[kind, ctx], ctx_right)
-        if way == 1:
-            return remote(kv.at[kind, ctx], kv.at[kind, ctx], kvs.at[kind, 1],
-                          kvr.at[kind, ctx], ctx_left)
-        b = before if kind == 0 else jnp.where(ctx == 0, 1, 0)
-        dev = ctx_right if kind == 0 else ctx_left
+    one, two = core, 1 - core
+
+    def kv_right(kind):
+        return remote(kv.at[kind, ctx], kv.at[kind, ctx], kvs.at[kind, 0], kvr.at[kind, ctx],
+                      ctx_right)
+
+    def kv_left(kind):
+        return remote(kv.at[kind, ctx], kv.at[kind, ctx], kvs.at[kind, 1], kvr.at[kind, ctx],
+                      ctx_left)
+
+    def kv_relay(kind, b, dev):
         return remote(kv.at[kind, b], kv.at[kind, b], kvs.at[kind, 2], kvr.at[kind, b], dev)
 
-    def kv_sends(kind, act):
-        left = ctx == 0 if kind == 0 else ctx <= 1
-
-        @pl.when(left)
-        def _():
-            act(kv_copy(kind, 1))
+    def kv_half(i, dev):
+        ref = kv.at[two, 0, i * (rows // 2) : (i + 1) * (rows // 2)]
+        return remote(ref, ref, kvs.at[two, 2], kvr.at[two, i * ZH], dev)
+
+    def kv_sends(first, act):
+        kind = one if first else two
+
+        @pl.when((ctx == 0) if first else (ctx <= 1))
+        def _():
+            act(kv_left(kind))
 
         @pl.when(ctx < ZH - 1)
         def _():
-            act(kv_copy(kind, 0))
-
-    def make(kind):
+            act(kv_right(kind))
+
+    def make(kind, first):
         if kind == 0:
             kv[0, ctx] = rotary(project(0, (0,)))
         else:
             kv[1, ctx] = project(0, (1,)).astype(jnp.bfloat16)
-        kv_sends(kind, lambda c: c.start())
+        kv_sends(first, lambda c: c.start())
 
     def arrived(kind, b):
         remote(kv.at[kind, b], kv.at[kind, b], kvs.at[kind, 0], kvr.at[kind, b],
@@ -261,18 +273,48 @@
     def docs_arrived(b):
         remote(docs.at[b], docs.at[b], ds.at[0], dr.at[b], ctx_right).wait_recv()
 
-    def relays():
+    def early_relays(act):
         @pl.when((ctx == 1) | (ctx == 2))
         def _():
+            act(doc_relay)
+
+        @pl.when(ctx == 2)
+        def _():
+            act(kv_relay(one, 1, ctx_right))
+
+        @pl.when(ctx == 3)
+        def _():
+            act(kv_relay(one, 0, ctx_left))
+
+        @pl.when(ctx == 0)
+        def _():
+            act(kv_relay(two, 1, ctx_left))
+
+    def late_relays(act):
+        @pl.when(ctx == 1)
+        def _():
+            act(kv_half(0, ctx_right))
+
+        @pl.when(ctx == 3)
+        def _():
+            act(kv_half(1, ctx_left))
+
+    def early_waits():
+        @pl.when((ctx == 1) | (ctx == 2))
+        def _():
             docs_arrived(before)
-            doc_relay.start()
-            arrived(0, before)
-            kv_copy(0, 2).start()
-
-        @pl.when((ctx == 0) | (ctx == 3))
-        def _():
-            arrived(1, jnp.where(ctx == 0, 1, 0))
-            kv_copy(1, 2).start()
+
+        @pl.when(ctx == 2)
+        def _():
+            arrived(one, 1)
+
+        @pl.when(ctx == 3)
+        def _():
+            arrived(one, 0)
+
+        @pl.when(ctx == 0)
+        def _():
+            arrived(two, 1)
 
     for cc in range(2):
 
@@ -281,6 +323,7 @@
             now, later_on = Gather(0, cc), Gather(1, cc)
             z_wait(0)
             now.start()
+            aside()
             now.own()
             for s in range(1, now.steps + 1):
                 now.relay(s)
@@ -288,13 +331,14 @@
             z_wait(2)
             later_on.start()
             hid_copy.wait()
-            make(cc)
+            make(cc, True)
             now.sibling_done()
-            make(1 - cc)
+            make(1 - cc, False)
             later_on.own()
             for s in range(1, later_on.steps + 1):
                 if s == later_on.steps:
-                    relays()
+                    early_waits()
+                    early_relays(lambda c: c.start())
                 later_on.relay(s)
             later_on.sibling_done()
             now.done()
@@ -334,17 +378,31 @@
 
     lax.fori_loop(0, HEADS, first, 0)
 
+    @pl.when((ctx == 1) | (ctx == 3))
+    def _():
+        arrived(two, 0)
+
+    late_relays(lambda c: c.start())
+
     def later(t, _):
         b = jnp.where(t == 0, ctx - 1, t - 1)
 
         @pl.when(jnp.logical_not(((ctx == 1) | (ctx == 2)) & (b == ctx - 1)))
         def _():
             docs_arrived(b)
-            arrived(0, b)
-
-        @pl.when(jnp.logical_not((ctx == 3) & (b == 0)))
-        def _():
-            arrived(1, b)
+
+        @pl.when(jnp.logical_not(((ctx == 2) & (b == 1)) | ((ctx == 3) & (b == 0))))
+        def _():
+            arrived(one, b)
+
+        @pl.when(b > 0)
+        def _():
+            arrived(two, b)
+
+        @pl.when((ctx == 2) & (b == 0))
+        def _():
+            kv_half(0, ctx_right).wait_recv()
+            kv_half(1, ctx_right).wait_recv()
 
         bias[...] = jnp.where(doc_query == docs[b].astype(jnp.float32), 0.0, -jnp.inf)
 
@@ -369,8 +427,10 @@
     for h in range(HEADS):
         out[:, h * HD : (h + 1) * HD] = (acc[h] / l_s[h]).astype(jnp.bfloat16)
 
-    for kind in range(2):
-        kv_sends(kind, lambda c: c.wait_send())
+    for first_sent in (True, False):
+        kv_sends(first_sent, lambda c: c.wait_send())
+    early_relays(lambda c: c.wait_send())
+    late_relays(lambda c: c.wait_send())
 
     @pl.when(ctx < ZH - 1)
     def _():
@@ -379,15 +439,6 @@
     @pl.when(ctx == 0)
     def _():
         doc_left.wait_send()
-
-    @pl.when((ctx == 1) | (ctx == 2))
-    def _():
-        doc_relay.wait_send()
-        kv_copy(0, 2).wait_send()
-
-    @pl.when((ctx == 0) | (ctx == 3))
-    def _():
-        kv_copy(1, 2).wait_send()
 
 
 def body(hidden_states, qkv_weight, doc_ids):
@@ -426,7 +477,7 @@
             dma((2,)),
             dma((2,)),
             dma((2, 3)),
-            dma((2, ZH)),
+            dma((2, ZH + 1)),
             dma((3,)),
             dma((ZH,)),
         ],

time: 78.2 us -> 73.5 us (0.940)
  the two profiles are of different devices: /device:TPU:769 before, /device:TPU:1 now
where the time goes in v3:
time: 73.5 us; the launch traced here: 73.3 us
  Pallas kernels  71.5 us (97%)
  local copies, waits for them, and re-layouts  1.77 us (2%)
    pallas_call x1, Pallas kernels, body(): pl.pallas_call(kernel, out_shape=jax.ShapeDtypeStruct((rows, HEADS * HD),...  71.5 us
    unnamed x1, local copies, waits for them, and re-layouts  1.77 us

profile of v3, /device:TPU:1, one launch (start us, length us, event | category | flops | bytes accessed | tf_op | source)
XLA Modules:
  0.0 73.3 jit_solution(6785431709098024419)
XLA Ops:
  0.0 71.5 %shard_map.37 = bf16[384,512]{1,0:T(8,128)(2,1)} custom-call(bf16[1,384,4096]{2,1,0:T(8,128)(2,1)} %hid.1, bf16[16,768]{1,0:T(8,128)(2,1)} %w_in.1, s32[1,384]{1,0:T(1,128)} %doc.1), custom_call_target="tpu_custom_call" | custom-call | tf_op jit(solution)/shard_map/pallas_call | solution.py:449
  71.5 1.8 %copy.5 = bf16[1,384,512]{2,1,0:T(8,128)(2,1)} copy(bf16[1,384,512]{2,1,0:T(8,128)(2,1)} %bitcast.1) | data formatting | bytes 786432

commit v4 on v3

--- a/solution.py
+++ b/solution.py
@@ -450,8 +450,8 @@
         kernel,
         out_shape=jax.ShapeDtypeStruct((rows, HEADS * HD), jnp.bfloat16),
         in_specs=[
-            pl.BlockSpec(memory_space=pl.ANY),
-            pl.BlockSpec(memory_space=pl.ANY),
+            pl.BlockSpec(memory_space=pltpu.HBM),
+            pl.BlockSpec(memory_space=pltpu.HBM),
             pl.BlockSpec(memory_space=pltpu.VMEM),
         ],
         out_specs=pl.BlockSpec(memory_space=pltpu.VMEM),
@@ -482,9 +482,9 @@
             dma((ZH,)),
         ],
         compiler_params=pltpu.CompilerParams(
-            collective_id=0, has_side_effects=True, vmem_limit_bytes=60 * 1024 * 1024
+            collective_id=0, has_side_effects=True, vmem_limit_bytes=24 * 1024 * 1024
         ),
-    )(hidden_states, qkv_weight, doc_ids)
+    )(pltpu.with_memory_space_constraint(hidden_states, pltpu.HBM), pltpu.with_memory_space_constraint(qkv_weight, pltpu.HBM), doc_ids)
     return result[None]
 
 

time: 73.5 us -> 72.2 us (0.982)
  Pallas kernels: 71.5 us -> 70.6 us
    pallas_call x1, Pallas kernels: 71.5 us -> 70.6 us  [body(): pl.pallas_call(kernel, out_shape=jax.ShapeDtypeStruct((rows, HEADS * HD),...]
    unnamed x1 -> x3, local copies, waits for them, and re-layouts: 1.77 us -> 1.43 us
where the time goes in v4:
time: 72.2 us; the launch traced here: 72 us
  Pallas kernels  70.6 us (98%)
  local copies, waits for them, and re-layouts  1.43 us (2%)
    pallas_call x1, Pallas kernels, body(): pl.pallas_call(kernel, out_shape=jax.ShapeDtypeStruct((rows, HEADS * HD),...  70.6 us

profile of v4, /device:TPU:1, one launch (start us, length us, event | category | flops | bytes accessed | tf_op | source)
XLA Modules:
  0.0 72.0 jit_solution(5880453454087419838)
XLA Ops:
  0.0 0.0 copy-start
  0.0 0.7 copy-done
  0.7 70.6 %shard_map.37 = bf16[384,512]{1,0:T(8,128)(2,1)S(1)} custom-call(bf16[1,384,4096]{2,1,0:T(8,128)(2,1)} %hid.1, bf16[16,768]{1,0:T(8,128)(2,1)} %w_in.1, s32[1,384]{1,0:T(1,128)S(1)} %copy-done), custom_call_target="tpu_custom_call" | custom-call | tf_op jit(solution)/shard_map/pallas_call | solution.py:449
  71.3 0.7 %copy.5 = bf16[1,384,512]{2,1,0:T(8,128)(2,1)} copy(bf16[1,384,512]{2,1,0:T(8,128)(2,1)S(1)} %bitcast.1) | data formatting | bytes 786432
Async XLA Ops:
  0.0 0.7 copy-start
